TPU v7x, 32 devices: a whole 2x2x4 slice. The times are simulated.
32 devices in a mesh: parts: 2 (over y), shard: 4 (over z), layer: 2 (over x), sub: 2 (over core).
Axes of the slice: x: 2, y: 2, z: 4, core: 2. Of those that a mesh axis runs over, the one named last changes fastest.
Arguments:
- act_in: bfloat16 [2, 1024, 14336], P('layer', ('parts', 'shard'), 'sub'), parts along dimension 1, may hold values from -6 to 6
- grad_out: bfloat16 [2, 1024, 8192], P('layer', ('parts', 'shard'), 'sub'), parts along dimension 1, may hold values from -6 to 6
- factor_in: bfloat16 [2, 12, 32, 14336], P('layer', 'shard', None, 'sub'), may hold values from -0.046875 to 0.046875
- factor_out: bfloat16 [2, 12, 32, 8192], P('layer', 'shard', None, 'sub'), may hold values from -0.0625 to 0.0625
- query_row: int32 [12], replicated, may hold values from 0 to 11, as said below
- pairs: int32 [2, 4, 12], replicated, may hold values from 0 to 1, as said below
Outputs:
- scores: float32 [1024, 12], P(('parts', 'shard'), 'layer'), parts along dimension 0
There are 2 independent parts, one for each index of `parts`. A program takes and returns all parts, laid end to end along the dimension named above; an argument that names none is the same for every part. Nothing has to cross between parts.
Inputs may be any that keep to these rules, and one draw needn't show every extreme that they name: A permutation: query q's factors are row query_row[q] of factor_in and factor_out. `pairs`: for each layer, shard and k, at most one listed query has its stored row in k * 3 to (k + 1) * 3 - 1; in every layer some shard lists one query for every k.
All inputs are finite; a program needn't handle non-finite values.
Results may differ from a plain program's by a relative error of at most 0.0003.
Values may be sent and summed in bfloat16 or wider, within the bound.
No kernel may reach another device: no remote copies, remote signals or barrier semaphores. Data moves between devices by JAX's collectives and lax.ppermute only.
A program may use at most 64 MiB of HBM per device.

v0:
```python
import functools

import jax
import jax.numpy as jnp
from jax import lax
from jax.experimental import pallas as pl
from jax.experimental.pallas import tpu as pltpu
from jax.sharding import PartitionSpec as P


def shifted(n, d):
    return [(i, (i + d) % n) for i in range(n)]


def wrap(i, n):
    return jnp.where(i >= n, i - n, i)


def dest(shard, j, n):
    if n & (n - 1) == 0:
        return shard ^ j
    return (shard + j) % n


def source(shard, j, n):
    if n & (n - 1) == 0:
        return shard ^ j
    return (shard + n - j) % n


def slot_groups(n):
    late = list(range(max(1, n // 2), n))
    return [j for j in range(n) if j not in late], late


def start_tables(query_hbm, pairs_hbm, query_row, pairs, sem):
    copies = [pltpu.make_async_copy(query_hbm, query_row, sem.at[0]), pltpu.make_async_copy(pairs_hbm, pairs, sem.at[1])]
    for copy in copies:
        copy.start()
    return copies


def table_scratch(query_row, pairs):
    return [pltpu.SMEM(query_row.shape, query_row.dtype), pltpu.SMEM(pairs.shape, pairs.dtype)]


def pick_rows(query_row, pairs, per_owner, dests):
    base = lax.axis_index("shard") * per_owner
    layer = lax.axis_index("layer")

    def step(q, rows):
        row = query_row[q] - base
        held = jnp.logical_and(row >= 0, row < per_owner)
        row = jnp.where(held, row, 0)
        return tuple(r + pairs[layer, to, q] * row for r, to in zip(rows, dests))

    count = query_row.shape[0]
    rows = lax.fori_loop(0, count, step, (jnp.int32(0),) * len(dests), unroll=count <= 16)
    return [jnp.clip(row, 0, per_owner - 1) for row in rows]


def span(part, wide):
    return pl.ds(pl.multiple_of(part * wide, 128), wide)


def send_kernel(parts, shard_count, query_hbm, pairs_hbm, act, grad, factor_in, factor_out, *refs):
    sent, (query_row, pairs, sem, table_sem) = refs[:-4], refs[-4:]
    tables = start_tables(query_hbm, pairs_hbm, query_row, pairs, table_sem)
    my_part, my_shard = lax.axis_index("parts"), lax.axis_index("shard")
    wide_out, wide_in = grad.shape[2] // parts, act.shape[2] // parts
    copies = []

    def start(source_out, source_in, target):
        for piece, place in ((source_out, pl.ds(0, wide_out)), (source_in, pl.ds(wide_out, wide_in))):
            copies.append(pltpu.make_async_copy(piece, target.at[:, place], sem.at[len(copies)]))
            copies[-1].start()

    for e in range(1, parts):
        part = wrap(my_part + e, parts)
        start(grad.at[0, :, span(part, wide_out)], act.at[0, :, span(part, wide_in)], sent[shard_count - 1 + e - 1])
    for table in tables:
        table.wait()
    dests = [dest(my_shard, j, shard_count) for j in range(1, shard_count)]
    for k, row in enumerate(pick_rows(query_row, pairs, factor_out.shape[1], dests)):
        start(factor_out.at[0, row, :, span(my_part, wide_out)], factor_in.at[0, row, :, span(my_part, wide_in)], sent[k])
    for copy in copies:
        copy.wait()


def make_sends(act, grad, factor_in, factor_out, query_row, pairs):
    parts, shard_count = lax.axis_size("parts"), lax.axis_size("shard")
    rank, tokens = factor_out.shape[2], act.shape[1]
    wide = (grad.shape[2] + act.shape[2]) // parts
    shapes = [pltpu.VMEM((rank, wide), act.dtype)] * (shard_count - 1)
    shapes += [pltpu.VMEM((tokens, wide), act.dtype)] * (parts - 1)
    sent = pl.pallas_call(
        functools.partial(send_kernel, parts, shard_count),
        out_shape=shapes,
        in_specs=[pl.BlockSpec(memory_space=pltpu.HBM)] * 6,
        out_specs=[pl.BlockSpec(memory_space=pltpu.VMEM)] * len(shapes),
        scratch_shapes=table_scratch(query_row, pairs)
        + [pltpu.SemaphoreType.DMA((2 * len(shapes),)), pltpu.SemaphoreType.DMA((2,))],
        compiler_params=pltpu.CompilerParams(vmem_limit_bytes=2**22),
        name="make_sends",
    )(query_row, pairs, act, grad, factor_in, factor_out)
    return sent[: shard_count - 1], sent[shard_count - 1 :]


def own_kernel(parts, order, query_hbm, pairs_hbm, act, grad, factor_in, factor_out, rows, slot, weights, *scratch):
    query_row, pairs, sem, table_sem = scratch
    tables = start_tables(query_hbm, pairs_hbm, query_row, pairs, table_sem)
    my_part, my_shard, my_layer = lax.axis_index("parts"), lax.axis_index("shard"), lax.axis_index("layer")
    layers, shard_count = lax.axis_size("layer"), lax.axis_size("shard")
    per_owner, tokens = factor_out.shape[1], rows.shape[0]
    wide_out, wide_in = grad.shape[2] // parts, act.shape[2] // parts
    span_out, span_in = span(my_part, wide_out), span(my_part, wide_in)
    to_out, to_in = pl.ds(0, wide_out), pl.ds(wide_out, wide_in)
    copies = [
        pltpu.make_async_copy(grad.at[0, :, span_out], rows.at[:, to_out], sem.at[0]),
        pltpu.make_async_copy(act.at[0, :, span_in], rows.at[:, to_in], sem.at[1]),
    ]
    for copy in copies:
        copy.start()
    for table in tables:
        table.wait()
    (row,) = pick_rows(query_row, pairs, per_owner, [my_shard])
    copies += [
        pltpu.make_async_copy(factor_out.at[0, row, :, span_out], slot.at[:, to_out], sem.at[2]),
        pltpu.make_async_copy(factor_in.at[0, row, :, span_in], slot.at[:, to_in], sem.at[3]),
    ]
    for copy in copies[2:]:
        copy.start()
    wide = query_row.shape[0] // layers
    for e in range(layers):
        layer = wrap(my_layer + e, layers)
        for i in range(wide):
            q = layer * wide + i
            listed = pairs[my_layer, my_shard, q]
            for k, j in enumerate(order):
                row = query_row[q] - source(my_shard, j, shard_count) * per_owner
                here = jnp.logical_and(row >= 0, row < per_owner)
                weight = jnp.where(here, listed, 0).astype(jnp.float32)
                weights[e, k, i : i + 1, :] = jnp.full((1, tokens), weight, jnp.float32)
    for copy in copies:
        copy.wait()


def make_own(order, act, grad, factor_in, factor_out, query_row, pairs):
    parts, layers = lax.axis_size("parts"), lax.axis_size("layer")
    rank, tokens = factor_out.shape[2], act.shape[1]
    wide = (grad.shape[2] + act.shape[2]) // parts
    shapes = [
        pltpu.VMEM((tokens, wide), act.dtype),
        pltpu.VMEM((rank, wide), act.dtype),
        pltpu.VMEM((layers, len(order), query_row.shape[0] // layers, tokens), jnp.float32),
    ]
    return pl.pallas_call(
        functools.partial(own_kernel, parts, tuple(order)),
        out_shape=shapes,
        in_specs=[pl.BlockSpec(memory_space=pltpu.HBM)] * 6,
        out_specs=[pl.BlockSpec(memory_space=pltpu.VMEM)] * len(shapes),
        scratch_shapes=table_scratch(query_row, pairs) + [pltpu.SemaphoreType.DMA((4,)), pltpu.SemaphoreType.DMA((2,))],
        compiler_params=pltpu.CompilerParams(vmem_limit_bytes=2**22),
        name="make_own",
    )(query_row, pairs, act, grad, factor_in, factor_out)


def project_kernel(slot_count, block_count, subs, wide_out, *refs):
    slots, blocks, rest = refs[:slot_count], refs[slot_count : slot_count + block_count], refs[slot_count + block_count :]
    carried, outs = rest[:-subs], rest[-subs:]
    my_sub = lax.axis_index("sub")
    dims = (((1,), (1,)), ((), ()))
    rank, wide = slots[0].shape
    half = rank // subs
    before = 0
    for k, old in enumerate(carried):
        before = old.shape[2]
        first = k // subs * old.shape[0]
        outs[k % subs][first : first + old.shape[0], :, :before] = old[...]
    for which, (low, high) in enumerate(((0, wide_out), (wide_out, wide))):
        left = jnp.concatenate([slot[:, low:high] for slot in slots], axis=0)
        for e, block in enumerate(blocks):
            proj = lax.dot_general(left, block[:, low:high], dims, preferred_element_type=jnp.float32)
            for j in range(slot_count):
                cuts = [proj[j * rank + c * half : j * rank + (c + 1) * half] for c in range(subs)]
                for f in range(subs):
                    sub = wrap(my_sub + f, subs)
                    cut = cuts[0]
                    for c in range(1, subs):
                        cut = jnp.where(sub == c, cuts[c], cut)
                    outs[f][e, which, before + j] = cut


def project(slots, blocks, wide_out, carried=()):
    subs = lax.axis_size("sub")
    vmem = pl.BlockSpec(memory_space=pltpu.VMEM)
    (rank, wide), tokens = slots[0].shape, blocks[0].shape[0]
    total = len(slots) + (carried[0].shape[2] if carried else 0)
    inputs = [pltpu.with_memory_space_constraint(x, pltpu.VMEM) for x in (*slots, *blocks, *carried)]
    flops = 2 * len(slots) * rank * len(blocks) * tokens * wide
    read = 2 * wide * (len(slots) * rank + len(blocks) * tokens)
    return pl.pallas_call(
        functools.partial(project_kernel, len(slots), len(blocks), subs, wide_out),
        out_shape=[pltpu.VMEM((len(blocks), 2, total, rank // subs, tokens), jnp.float32)] * subs,
        in_specs=[vmem] * len(inputs),
        out_specs=[vmem] * subs,
        compiler_params=pltpu.CompilerParams(vmem_limit_bytes=2**23),
        cost_estimate=pl.CostEstimate(flops=flops, bytes_accessed=read, transcendentals=0),
        name="project",
    )(*inputs)


def score_kernel(here_count, weights, *refs):
    slot_count = weights.shape[1]
    pieces, out = refs[:-1], refs[-1]
    total = pieces[0][0]
    for k, piece in enumerate(pieces[1:]):
        total = total + (piece[0] if k + 1 < here_count else piece[...])
    scores = [jnp.sum(total[0, k] * total[1, k], axis=0, keepdims=True) for k in range(slot_count)]
    for e in range(weights.shape[0]):
        block = weights[e, 0] * scores[0]
        for k in range(1, slot_count):
            block = block + weights[e, k] * scores[k]
        out[e] = block


def make_scores(weights, here, far):
    layers, _, wide, tokens = weights.shape
    vmem = pl.BlockSpec(memory_space=pltpu.VMEM)
    inputs = [pltpu.with_memory_space_constraint(x, pltpu.VMEM) for x in (weights, *here, *far)]
    return pl.pallas_call(
        functools.partial(score_kernel, len(here)),
        out_shape=pltpu.VMEM((layers, wide, tokens), jnp.float32),
        in_specs=[vmem] * len(inputs),
        out_specs=vmem,
        compiler_params=pltpu.CompilerParams(vmem_limit_bytes=2**23),
        name="make_scores",
    )(*inputs)


def shards(act_in, grad_out, factor_in, factor_out, query_row, pairs):
    parts = lax.axis_size("parts")
    shard_count = lax.axis_size("shard")
    layers = lax.axis_size("layer")
    subs = lax.axis_size("sub")
    wide_out = grad_out.shape[2] // parts
    early, late = slot_groups(shard_count)

    args = [
        pltpu.with_memory_space_constraint(x, pltpu.HBM)
        for x in (act_in, grad_out, factor_in, factor_out, query_row, pairs)
    ]
    sent_slots, sent_rows = make_sends(*args)
    rows = []
    for e in range(1, parts):
        rows.append(lax.ppermute(sent_rows[e - 1], "parts", shifted(parts, e)))
    slots = [None] * shard_count
    for j in late[::-1] + early[1:]:
        to = [(i, dest(i, j, shard_count)) for i in range(shard_count)]
        slots[j] = lax.ppermute(sent_slots[j - 1], "shard", to)
    own_rows, slots[0], weights = make_own(early + late, *args)

    early_own = project([slots[j] for j in early], [own_rows], wide_out)
    early_rest = project([slots[j] for j in early], rows, wide_out) if rows else []
    cuts = project([slots[j] for j in late], [own_rows] + rows, wide_out, list(early_own) + list(early_rest))

    got = [lax.ppermute(cuts[f], "sub", shifted(subs, f)) for f in range(1, subs)]
    far = []
    for e in range(1, parts):
        total = cuts[0][e]
        for piece in got:
            total = total + piece[e]
        far.append(lax.ppermute(total, "parts", shifted(parts, parts - e)))
    blocks = make_scores(weights, [cuts[0]] + got, far)

    if subs == 2:
        blocks = blocks + lax.ppermute(blocks, "sub", shifted(subs, 1))
    else:
        blocks = lax.psum(blocks, "sub")
    out = blocks[0]
    for e in range(1, layers):
        out = out + lax.ppermute(blocks[e], "layer", shifted(layers, e))
    return out.T


def solution(mesh):
    in_specs = (
        P("layer", ("parts", "shard"), "sub"),
        P("layer", ("parts", "shard"), "sub"),
        P("layer", "shard", None, "sub"),
        P("layer", "shard", None, "sub"),
        P(),
        P(),
    )
    out_specs = P(("parts", "shard"), "layer")

    return jax.shard_map(shards, mesh=mesh, in_specs=in_specs, out_specs=out_specs, check_vma=False)
```

profile of v0, /device:TPU:0, one launch (start us, length us, event | category | flops | bytes accessed | tf_op | source)
XLA Modules:
  0.0 50.0 jit_solution(2099642608649825281)
XLA Ops:
  0.0 2.2 %make_sends.1 = (bf16[32,5632]{1,0:T(8,128)(2,1)S(1)}, bf16[32,5632]{1,0:T(8,128)(2,1)S(1)}, bf16[32,5632]{1,0:T(8,128)(2,1)S(1)}, bf16[128,5632]{1,0:T(8,128)(2,1)S(1)}) custom-call(s32[12]{0:T(128)} %query_hbm.3, s32[2,4,12]{2,1,0:T(4,128)} %pairs_hbm.3, bf16[1,128,7168]{2,1,0:T(8,128)(2,1)} %act.3, bf16[1,128,4096]{2,1,0:T(8,128)(2,1)} %grad.3, ...), custom_call_target="tpu_custom_call" | custom-call | tf_op jit(solution)/shard_map/make_sends/pallas_call | solution.py:96
  2.2 3.2 %collective-permute-start.2 = (bf16[128,5632]{1,0:T(8,128)(2,1)S(1)}, bf16[128,5632]{1,0:T(8,128)(2,1)S(1)}, u32[]{:S(2)}, u32[]{:S(2)}) collective-permute-start(bf16[128,5632]{1,0:T(8,128)(2,1)S(1)} %get-tuple-element.22), channel_id=1, source_target_pairs={{0,16},{16,0},{1,17},{17,1},{2,18},{18,2},{3,19},{19,3},{4,20},{20... | collective-permute-start | bytes 4325384 | tf_op jit(solution)/shard_map/ppermute | solution.py:256
  5.5 1.3 %collective-permute-start.3 = (bf16[32,5632]{1,0:T(8,128)(2,1)S(1)}, bf16[32,5632]{1,0:T(8,128)(2,1)S(1)}, u32[]{:S(2)}, u32[]{:S(2)}) collective-permute-start(bf16[32,5632]{1,0:T(8,128)(2,1)S(1)} %get-tuple-element.24), channel_id=1, source_target_pairs={{0,4},{4,0},{8,12},{12,8},{1,5},{5,1},{9,13},{13,9},{2,6},{6,2},{1... | collective-permute-start | bytes 1081352 | tf_op jit(solution)/shard_map/ppermute | solution.py:260
  6.8 2.6 %collective-permute-start = (bf16[32,5632]{1,0:T(8,128)(2,1)S(1)}, bf16[32,5632]{1,0:T(8,128)(2,1)S(1)}, u32[]{:S(2)}, u32[]{:S(2)}) collective-permute-start(bf16[32,5632]{1,0:T(8,128)(2,1)S(1)} %get-tuple-element.19), channel_id=1, source_target_pairs={{0,8},{4,12},{8,0},{12,4},{1,9},{5,13},{9,1},{13,5},{2,10},{6,14},... | collective-permute-start | bytes 1081352 | tf_op jit(solution)/shard_map/ppermute | solution.py:260
  9.4 0.5 collective-permute-start.1
  9.9 1.9 %make_own.1 = (bf16[128,5632]{1,0:T(8,128)(2,1)S(1)}, bf16[32,5632]{1,0:T(8,128)(2,1)S(1)}, f32[2,4,6,128]{3,2,1,0:T(8,128)S(1)}) custom-call(s32[12]{0:T(128)} %query_hbm.3, s32[2,4,12]{2,1,0:T(4,128)} %pairs_hbm.3, bf16[1,128,7168]{2,1,0:T(8,128)(2,1)} %act.3, bf16[1,128,4096]{2,1,0:T(8,128)(2,1)} %grad.3, bf16[1,3,32,7168]{3,2,1,0:T(8,128)(2,1)} %factor_in.3, ...), custom_call_target="tpu_custom_call" | custom-call | tf_op jit(solution)/shard_map/make_own/pallas_call | solution.py:157
  11.8 10.4 %collective-permute-done.3.refs_1_ = bf16[32,5632]{1,0:T(8,128)(2,1)S(1)} collective-permute-done((bf16[32,5632]{1,0:T(8,128)(2,1)S(1)}, bf16[32,5632]{1,0:T(8,128)(2,1)S(1)}, u32[]{:S(2)}, u32[]{:S(2)}) %collective-permute-start.3) | collective-permute-done | bytes 360480 | tf_op jit(solution)/shard_map/ppermute | solution.py:260
  22.2 0.6 %project.3 = (f32[1,2,2,16,128]{4,3,2,1,0:T(8,128)S(1)}, f32[1,2,2,16,128]{4,3,2,1,0:T(8,128)S(1)}) custom-call(bf16[32,5632]{1,0:T(8,128)(2,1)S(1)} %get-tuple-element.23.refs_0_, bf16[32,5632]{1,0:T(8,128)(2,1)S(1)} %collective-permute-done.3.refs_1_, bf16[128,5632]{1,0:T(8,128)(2,1)S(1)} %get-tuple-element.21.refs_2_), custom_call_target="tpu_custom_call" | custom-call | flops 92274688 | bytes 2162688 | tf_op jit(solution)/shard_map/project/pallas_call | solution.py:202
  22.8 14.3 %collective-permute-done.2.refs_2_.refs_3_ = bf16[128,5632]{1,0:T(8,128)(2,1)S(1)} collective-permute-done((bf16[128,5632]{1,0:T(8,128)(2,1)S(1)}, bf16[128,5632]{1,0:T(8,128)(2,1)S(1)}, u32[]{:S(2)}, u32[]{:S(2)}) %collective-permute-start.2) | collective-permute-done | bytes 1441824 | tf_op jit(solution)/shard_map/ppermute | solution.py:256
  37.1 0.6 %project.4 = (f32[1,2,2,16,128]{4,3,2,1,0:T(8,128)S(1)}, f32[1,2,2,16,128]{4,3,2,1,0:T(8,128)S(1)}) custom-call(bf16[32,5632]{1,0:T(8,128)(2,1)S(1)} %get-tuple-element.23.refs_0_, bf16[32,5632]{1,0:T(8,128)(2,1)S(1)} %collective-permute-done.3.refs_1_, bf16[128,5632]{1,0:T(8,128)(2,1)S(1)} %collective-permute-done.2.refs_2_.refs_3_), custom_call_target="tpu_custom_call" | custom-call | flops 92274688 | bytes 2162688 | tf_op jit(solution)/shard_map/project/pallas_call | solution.py:202
  37.7 0.0 collective-permute-done.refs_0_
  37.7 0.0 collective-permute-done.1.refs_1_
  37.7 1.1 %project.5 = (f32[2,2,4,16,128]{4,3,2,1,0:T(8,128)S(1)}, f32[2,2,4,16,128]{4,3,2,1,0:T(8,128)S(1)}) custom-call(bf16[32,5632]{1,0:T(8,128)(2,1)S(1)} %collective-permute-done.refs_0_, bf16[32,5632]{1,0:T(8,128)(2,1)S(1)} %collective-permute-done.1.refs_1_, bf16[128,5632]{1,0:T(8,128)(2,1)S(1)} %get-tuple-element.21.refs_2_, ...), custom_call_target="tpu_custom_call" | custom-call | flops 184549376 | bytes 3604480 | tf_op jit(solution)/shard_map/project/pallas_call | solution.py:202
  38.8 0.1 collective-permute-start.4
  38.8 1.3 %collective-permute-done.4.refs_1_ = f32[2,2,4,16,128]{4,3,2,1,0:T(8,128)S(1)} collective-permute-done((f32[2,2,4,16,128]{4,3,2,1,0:T(8,128)S(1)}, f32[2,2,4,16,128]{4,3,2,1,0:T(8,128)S(1)}, u32[]{:S(2)}, u32[]{:S(2)}) %collective-permute-start.4) | collective-permute-done | bytes 131104 | tf_op jit(solution)/shard_map/ppermute | solution.py:267
  40.2 1.8 %collective-permute-start.5 = (f32[2,4,16,128]{3,2,1,0:T(8,128)S(1)}, f32[2,4,16,128]{3,2,1,0:T(8,128)S(1)}, u32[]{:S(2)}, u32[]{:S(2)}) collective-permute-start(f32[2,4,16,128]{3,2,1,0:T(8,128)S(1)} %fusion), channel_id=1, source_target_pairs={{0,16},{16,0},{1,17},{17,1},{2,18},{18,2},{3,19},{19,3},{4,20},{20... | collective-permute-start | bytes 196616 | tf_op jit(solution)/shard_map/ppermute | solution.py:273
  42.0 2.5 %collective-permute-done.5.refs_2_ = f32[2,4,16,128]{3,2,1,0:T(8,128)S(1)} collective-permute-done((f32[2,4,16,128]{3,2,1,0:T(8,128)S(1)}, f32[2,4,16,128]{3,2,1,0:T(8,128)S(1)}, u32[]{:S(2)}, u32[]{:S(2)}) %collective-permute-start.5) | collective-permute-done | bytes 65568 | tf_op jit(solution)/shard_map/ppermute | solution.py:273
  44.6 0.1 collective-permute-start.6
  44.6 1.2 %collective-permute-done.6 = f32[2,6,128]{2,1,0:T(8,128)S(1)} collective-permute-done((f32[2,6,128]{2,1,0:T(8,128)S(1)}, f32[2,6,128]{2,1,0:T(8,128)S(1)}, u32[]{:S(2)}, u32[]{:S(2)}) %collective-permute-start.6) | collective-permute-done | bytes 6176 | tf_op jit(solution)/shard_map/ppermute | solution.py:277
  45.8 1.5 %collective-permute-start.7 = (f32[6,128]{1,0:T(8,128)S(1)}, f32[6,128]{1,0:T(8,128)S(1)}, u32[]{:S(2)}, u32[]{:S(2)}) collective-permute-start(f32[6,128]{1,0:T(8,128)S(1)} %slice_bitcast_fusion), channel_id=1, source_target_pairs={{0,2},{2,0},{1,3},{3,1},{4,6},{6,4},{5,7},{7,5},{8,10},{10,8},{9,1... | collective-permute-start | bytes 9224 | tf_op jit(solution)/shard_map/ppermute | solution.py:282
  47.3 2.1 %collective-permute-done.7 = f32[6,128]{1,0:T(8,128)S(1)} collective-permute-done((f32[6,128]{1,0:T(8,128)S(1)}, f32[6,128]{1,0:T(8,128)S(1)}, u32[]{:S(2)}, u32[]{:S(2)}) %collective-permute-start.7) | collective-permute-done | bytes 3104 | tf_op jit(solution)/shard_map/ppermute | solution.py:282
  49.4 0.6 %fusion.2 = f32[128,6]{0,1:T(8,128)} fusion(f32[6,128]{1,0:T(8,128)S(1)} %collective-permute-done.7, f32[2,6,128]{2,1,0:T(8,128)S(1)} %add.14), kind=kLoop, calls=%fused_computation.5 | loop fusion | flops 768 | bytes 9216 | tf_op jit(solution)/shard_map/transpose | solution.py:283
  (4 shorter events, 0.0 us)
Async XLA Ops:
  2.2 34.8 %collective-permute-start.2 = (bf16[128,5632]{1,0:T(8,128)(2,1)S(1)}, bf16[128,5632]{1,0:T(8,128)(2,1)S(1)}, u32[]{:S(2)}, u32[]{:S(2)}) collective-permute-start(bf16[128,5632]{1,0:T(8,128)(2,1)S(1)} %get-tuple-element.22), channel_id=1, source_target_pairs={{0,16},{16,0},{1,17},{17,1},{2,18},{18,2},{3,19},{19,3},{4,20},{20... | collective-permute-start | bytes 4325384 | tf_op jit(solution)/shard_map/ppermute | solution.py:256
  5.5 16.7 %collective-permute-start.3 = (bf16[32,5632]{1,0:T(8,128)(2,1)S(1)}, bf16[32,5632]{1,0:T(8,128)(2,1)S(1)}, u32[]{:S(2)}, u32[]{:S(2)}) collective-permute-start(bf16[32,5632]{1,0:T(8,128)(2,1)S(1)} %get-tuple-element.24), channel_id=1, source_target_pairs={{0,4},{4,0},{8,12},{12,8},{1,5},{5,1},{9,13},{13,9},{2,6},{6,2},{1... | collective-permute-start | bytes 1081352 | tf_op jit(solution)/shard_map/ppermute | solution.py:260
  6.8 30.8 %collective-permute-start = (bf16[32,5632]{1,0:T(8,128)(2,1)S(1)}, bf16[32,5632]{1,0:T(8,128)(2,1)S(1)}, u32[]{:S(2)}, u32[]{:S(2)}) collective-permute-start(bf16[32,5632]{1,0:T(8,128)(2,1)S(1)} %get-tuple-element.19), channel_id=1, source_target_pairs={{0,8},{4,12},{8,0},{12,4},{1,9},{5,13},{9,1},{13,5},{2,10},{6,14},... | collective-permute-start | bytes 1081352 | tf_op jit(solution)/shard_map/ppermute | solution.py:260
  9.4 28.3 %collective-permute-start.1 = (bf16[32,5632]{1,0:T(8,128)(2,1)S(1)}, bf16[32,5632]{1,0:T(8,128)(2,1)S(1)}, u32[]{:S(2)}, u32[]{:S(2)}) collective-permute-start(bf16[32,5632]{1,0:T(8,128)(2,1)S(1)} %get-tuple-element.20), channel_id=1, source_target_pairs={{0,12},{4,8},{8,4},{12,0},{1,13},{5,9},{9,5},{13,1},{2,14},{6,10},... | collective-permute-start | bytes 1081352 | tf_op jit(solution)/shard_map/ppermute | solution.py:260
  38.8 1.4 %collective-permute-start.4 = (f32[2,2,4,16,128]{4,3,2,1,0:T(8,128)S(1)}, f32[2,2,4,16,128]{4,3,2,1,0:T(8,128)S(1)}, u32[]{:S(2)}, u32[]{:S(2)}) collective-permute-start(f32[2,2,4,16,128]{4,3,2,1,0:T(8,128)S(1)} %get-tuple-element.30), channel_id=1, source_target_pairs={{0,1},{1,0},{2,3},{3,2},{4,5},{5,4},{6,7},{7,6},{8,9},{9,8},{10,11... | collective-permute-start | bytes 393224 | tf_op jit(solution)/shard_map/ppermute | solution.py:267
  40.2 4.3 %collective-permute-start.5 = (f32[2,4,16,128]{3,2,1,0:T(8,128)S(1)}, f32[2,4,16,128]{3,2,1,0:T(8,128)S(1)}, u32[]{:S(2)}, u32[]{:S(2)}) collective-permute-start(f32[2,4,16,128]{3,2,1,0:T(8,128)S(1)} %fusion), channel_id=1, source_target_pairs={{0,16},{16,0},{1,17},{17,1},{2,18},{18,2},{3,19},{19,3},{4,20},{20... | collective-permute-start | bytes 196616 | tf_op jit(solution)/shard_map/ppermute | solution.py:273
  44.6 1.2 %collective-permute-start.6 = (f32[2,6,128]{2,1,0:T(8,128)S(1)}, f32[2,6,128]{2,1,0:T(8,128)S(1)}, u32[]{:S(2)}, u32[]{:S(2)}) collective-permute-start(f32[2,6,128]{2,1,0:T(8,128)S(1)} %make_scores.1), channel_id=1, source_target_pairs={{0,1},{1,0},{2,3},{3,2},{4,5},{5,4},{6,7},{7,6},{8,9},{9,8},{10,11... | collective-permute-start | bytes 18440 | tf_op jit(solution)/shard_map/ppermute | solution.py:277
  45.8 3.6 %collective-permute-start.7 = (f32[6,128]{1,0:T(8,128)S(1)}, f32[6,128]{1,0:T(8,128)S(1)}, u32[]{:S(2)}, u32[]{:S(2)}) collective-permute-start(f32[6,128]{1,0:T(8,128)S(1)} %slice_bitcast_fusion), channel_id=1, source_target_pairs={{0,2},{2,0},{1,3},{3,1},{4,6},{6,4},{5,7},{7,5},{8,10},{10,8},{9,1... | collective-permute-start | bytes 9224 | tf_op jit(solution)/shard_map/ppermute | solution.py:282
where the time goes:
time: 50.5 us; the launch traced here: 50 us
  waiting for transfers between devices  31.8 us (63%)
  starting transfers between devices  11 us (22%)
  Pallas kernels  6.44 us (13%)
  other arithmetic  0.61 us (1%)
    ppermute x1, waiting for transfers between devices, shards(): rows.append(lax.ppermute(sent_rows[e - 1], 'parts', shifted(parts, e)))  14.3 us
    ppermute x3, waiting for transfers between devices, shards(): slots[j] = lax.ppermute(sent_slots[j - 1], 'shard', to)  10.4 us
    ppermute x3, starting transfers between devices, shards(): slots[j] = lax.ppermute(sent_slots[j - 1], 'shard', to)  4.39 us
    ppermute x1, starting transfers between devices, shards(): rows.append(lax.ppermute(sent_rows[e - 1], 'parts', shifted(parts, e)))  3.22 us
    ppermute x1, waiting for transfers between devices, shards(): far.append(lax.ppermute(total, 'parts', shifted(parts, parts - e)))  2.52 us
    pallas_call x3, Pallas kernels, project(): pl.pallas_call(functools.partial(project_kernel, len(slots), len(blocks),...  2.27 us
    pallas_call x1, Pallas kernels, make_sends(): pl.pallas_call(functools.partial(send_kernel, parts, shard_count), out_sh...  2.24 us
    ppermute x1, waiting for transfers between devices, shards(): out = out + lax.ppermute(blocks[e], 'layer', shifted(layers, e))  2.13 us
  transfers between devices with their start and end apart: 8, of which 6 were waited for; matrix products, arithmetic and copies ran while one was open for 0% of the time, Pallas kernels for 6%

commit v1 on v0

--- a/solution.py
+++ b/solution.py
@@ -1,4 +1,5 @@
 import functools
+import itertools
 
 import jax
 import jax.numpy as jnp
@@ -8,8 +9,11 @@
 from jax.sharding import PartitionSpec as P
 
 
-def shifted(n, d):
-    return [(i, (i + d) % n) for i in range(n)]
+def shifted(sizes, shift):
+    places = list(itertools.product(*[range(n) for n in sizes]))
+    return [
+        (i, places.index(tuple((a + b) % n for a, b, n in zip(place, shift, sizes)))) for i, place in enumerate(places)
+    ]
 
 
 def wrap(i, n):
@@ -64,26 +68,32 @@
 
 
 def send_kernel(parts, shard_count, query_hbm, pairs_hbm, act, grad, factor_in, factor_out, *refs):
-    sent, (query_row, pairs, sem, table_sem) = refs[:-4], refs[-4:]
+    sent, (query_row, pairs, stored, sem, table_sem) = refs[:-5], refs[-5:]
     tables = start_tables(query_hbm, pairs_hbm, query_row, pairs, table_sem)
     my_part, my_shard = lax.axis_index("parts"), lax.axis_index("shard")
     wide_out, wide_in = grad.shape[2] // parts, act.shape[2] // parts
+    to_out, to_in = pl.ds(0, wide_out), pl.ds(wide_out, wide_in)
     copies = []
 
-    def start(source_out, source_in, target):
-        for piece, place in ((source_out, pl.ds(0, wide_out)), (source_in, pl.ds(wide_out, wide_in))):
-            copies.append(pltpu.make_async_copy(piece, target.at[:, place], sem.at[len(copies)]))
-            copies[-1].start()
-
+    def start(piece, target):
+        copies.append(pltpu.make_async_copy(piece, target, sem.at[len(copies)]))
+        copies[-1].start()
+
+    start(factor_out.at[0, :, :, span(my_part, wide_out)], stored.at[:, :, to_out])
+    start(factor_in.at[0, :, :, span(my_part, wide_in)], stored.at[:, :, to_in])
     for e in range(1, parts):
         part = wrap(my_part + e, parts)
-        start(grad.at[0, :, span(part, wide_out)], act.at[0, :, span(part, wide_in)], sent[shard_count - 1 + e - 1])
+        start(grad.at[0, :, span(part, wide_out)], sent[shard_count - 1 + e - 1].at[:, to_out])
+        start(act.at[0, :, span(part, wide_in)], sent[shard_count - 1 + e - 1].at[:, to_in])
     for table in tables:
         table.wait()
     dests = [dest(my_shard, j, shard_count) for j in range(1, shard_count)]
-    for k, row in enumerate(pick_rows(query_row, pairs, factor_out.shape[1], dests)):
-        start(factor_out.at[0, row, :, span(my_part, wide_out)], factor_in.at[0, row, :, span(my_part, wide_in)], sent[k])
-    for copy in copies:
+    listed = pick_rows(query_row, pairs, factor_out.shape[1], dests)
+    for copy in copies[:2]:
+        copy.wait()
+    for target, row in zip(sent, listed):
+        target[...] = stored[row]
+    for copy in copies[2:]:
         copy.wait()
 
 
@@ -99,8 +109,12 @@
         in_specs=[pl.BlockSpec(memory_space=pltpu.HBM)] * 6,
         out_specs=[pl.BlockSpec(memory_space=pltpu.VMEM)] * len(shapes),
         scratch_shapes=table_scratch(query_row, pairs)
-        + [pltpu.SemaphoreType.DMA((2 * len(shapes),)), pltpu.SemaphoreType.DMA((2,))],
-        compiler_params=pltpu.CompilerParams(vmem_limit_bytes=2**22),
+        + [
+            pltpu.VMEM((factor_out.shape[1], rank, wide), act.dtype),
+            pltpu.SemaphoreType.DMA((2 * parts,)),
+            pltpu.SemaphoreType.DMA((2,)),
+        ],
+        compiler_params=pltpu.CompilerParams(vmem_limit_bytes=2**23),
         name="make_sends",
     )(query_row, pairs, act, grad, factor_in, factor_out)
     return sent[: shard_count - 1], sent[shard_count - 1 :]
@@ -167,16 +181,13 @@
 
 def project_kernel(slot_count, block_count, subs, wide_out, *refs):
     slots, blocks, rest = refs[:slot_count], refs[slot_count : slot_count + block_count], refs[slot_count + block_count :]
-    carried, outs = rest[:-subs], rest[-subs:]
+    carried, outs = rest[: -block_count * subs], rest[-block_count * subs :]
     my_sub = lax.axis_index("sub")
     dims = (((1,), (1,)), ((), ()))
     rank, wide = slots[0].shape
     half = rank // subs
-    before = 0
-    for k, old in enumerate(carried):
-        before = old.shape[2]
-        first = k // subs * old.shape[0]
-        outs[k % subs][first : first + old.shape[0], :, :before] = old[...]
+    for out, old in zip(outs, carried):
+        out[:, : old.shape[1]] = old[...]
     for which, (low, high) in enumerate(((0, wide_out), (wide_out, wide))):
         left = jnp.concatenate([slot[:, low:high] for slot in slots], axis=0)
         for e, block in enumerate(blocks):
@@ -188,51 +199,60 @@
                     cut = cuts[0]
                     for c in range(1, subs):
                         cut = jnp.where(sub == c, cuts[c], cut)
-                    outs[f][e, which, before + j] = cut
+                    out = outs[e * subs + f]
+                    out[which, out.shape[1] - slot_count + j] = cut
 
 
 def project(slots, blocks, wide_out, carried=()):
     subs = lax.axis_size("sub")
     vmem = pl.BlockSpec(memory_space=pltpu.VMEM)
     (rank, wide), tokens = slots[0].shape, blocks[0].shape[0]
-    total = len(slots) + (carried[0].shape[2] if carried else 0)
+    counts = [len(slots) + (carried[k].shape[1] if k < len(carried) else 0) for k in range(len(blocks) * subs)]
     inputs = [pltpu.with_memory_space_constraint(x, pltpu.VMEM) for x in (*slots, *blocks, *carried)]
     flops = 2 * len(slots) * rank * len(blocks) * tokens * wide
     read = 2 * wide * (len(slots) * rank + len(blocks) * tokens)
     return pl.pallas_call(
         functools.partial(project_kernel, len(slots), len(blocks), subs, wide_out),
-        out_shape=[pltpu.VMEM((len(blocks), 2, total, rank // subs, tokens), jnp.float32)] * subs,
+        out_shape=[pltpu.VMEM((2, count, rank // subs, tokens), jnp.float32) for count in counts],
         in_specs=[vmem] * len(inputs),
-        out_specs=[vmem] * subs,
+        out_specs=[vmem] * len(counts),
         compiler_params=pltpu.CompilerParams(vmem_limit_bytes=2**23),
         cost_estimate=pl.CostEstimate(flops=flops, bytes_accessed=read, transcendentals=0),
         name="project",
     )(*inputs)
 
 
-def score_kernel(here_count, weights, *refs):
-    slot_count = weights.shape[1]
-    pieces, out = refs[:-1], refs[-1]
-    total = pieces[0][0]
-    for k, piece in enumerate(pieces[1:]):
-        total = total + (piece[0] if k + 1 < here_count else piece[...])
-    scores = [jnp.sum(total[0, k] * total[1, k], axis=0, keepdims=True) for k in range(slot_count)]
-    for e in range(weights.shape[0]):
+def score_kernel(counts, weights, *refs):
+    pieces, outs = list(refs[: sum(counts)]), refs[sum(counts) :]
+    whole = [pieces.pop(0) for _ in range(counts[0])]
+    scores = []
+    for count in counts[1:]:
+        parted = [pieces.pop(0) for _ in range(count)]
+        width = parted[0].shape[1]
+        total = whole[0][:, len(scores) : len(scores) + width]
+        for piece in whole[1:]:
+            total = total + piece[:, len(scores) : len(scores) + width]
+        for piece in parted:
+            total = total + piece[...]
+        scores += [jnp.sum(total[0, k] * total[1, k], axis=0, keepdims=True) for k in range(width)]
+    for e, out in enumerate(outs):
         block = weights[e, 0] * scores[0]
-        for k in range(1, slot_count):
+        for k in range(1, len(scores)):
             block = block + weights[e, k] * scores[k]
-        out[e] = block
-
-
-def make_scores(weights, here, far):
+        out[...] = block
+
+
+def make_scores(weights, whole, parted):
     layers, _, wide, tokens = weights.shape
     vmem = pl.BlockSpec(memory_space=pltpu.VMEM)
-    inputs = [pltpu.with_memory_space_constraint(x, pltpu.VMEM) for x in (weights, *here, *far)]
+    pieces = [weights, *whole] + [piece for group in parted for piece in group]
+    inputs = [pltpu.with_memory_space_constraint(x, pltpu.VMEM) for x in pieces]
+    counts = (len(whole), *[len(group) for group in parted])
     return pl.pallas_call(
-        functools.partial(score_kernel, len(here)),
-        out_shape=pltpu.VMEM((layers, wide, tokens), jnp.float32),
+        functools.partial(score_kernel, counts),
+        out_shape=[pltpu.VMEM((wide, tokens), jnp.float32)] * layers,
         in_specs=[vmem] * len(inputs),
-        out_specs=vmem,
+        out_specs=[vmem] * layers,
         compiler_params=pltpu.CompilerParams(vmem_limit_bytes=2**23),
         name="make_scores",
     )(*inputs)
@@ -253,33 +273,35 @@
     sent_slots, sent_rows = make_sends(*args)
     rows = []
     for e in range(1, parts):
-        rows.append(lax.ppermute(sent_rows[e - 1], "parts", shifted(parts, e)))
+        rows.append(lax.ppermute(sent_rows[e - 1], "parts", shifted((parts,), (e,))))
     slots = [None] * shard_count
     for j in late[::-1] + early[1:]:
         to = [(i, dest(i, j, shard_count)) for i in range(shard_count)]
         slots[j] = lax.ppermute(sent_slots[j - 1], "shard", to)
     own_rows, slots[0], weights = make_own(early + late, *args)
 
+    def give_back(cuts):
+        got = []
+        for k, cut in enumerate(cuts):
+            e, f = 1 + k // subs, k % subs
+            got.append(lax.ppermute(cut, ("parts", "sub"), shifted((parts, subs), (parts - e, f))))
+        return got
+
     early_own = project([slots[j] for j in early], [own_rows], wide_out)
-    early_rest = project([slots[j] for j in early], rows, wide_out) if rows else []
-    cuts = project([slots[j] for j in late], [own_rows] + rows, wide_out, list(early_own) + list(early_rest))
-
-    got = [lax.ppermute(cuts[f], "sub", shifted(subs, f)) for f in range(1, subs)]
-    far = []
-    for e in range(1, parts):
-        total = cuts[0][e]
-        for piece in got:
-            total = total + piece[e]
-        far.append(lax.ppermute(total, "parts", shifted(parts, parts - e)))
-    blocks = make_scores(weights, [cuts[0]] + got, far)
-
-    if subs == 2:
-        blocks = blocks + lax.ppermute(blocks, "sub", shifted(subs, 1))
-    else:
-        blocks = lax.psum(blocks, "sub")
-    out = blocks[0]
-    for e in range(1, layers):
-        out = out + lax.ppermute(blocks[e], "layer", shifted(layers, e))
+    early_rest = project([slots[j] for j in early], rows, wide_out)
+    early_got = give_back(early_rest)
+    cuts = project([slots[j] for j in late], [own_rows] + rows, wide_out, early_own)
+    late_got = give_back(cuts[subs:])
+    whole = [cuts[0]]
+    for f in range(1, subs):
+        whole.append(lax.ppermute(cuts[f], "sub", shifted((subs,), (f,))))
+    blocks = make_scores(weights, whole, [early_got, late_got])
+
+    out = None
+    for e in range(layers):
+        terms = [blocks[0] if e == f == 0 else lax.ppermute(blocks[e], ("layer", "sub"), shifted((layers, subs), (e, f))) for f in range(subs)]
+        total = sum(terms[1:], terms[0])
+        out = total if out is None else out + total
     return out.T
 
 

time: 50.5 us -> 51.2 us (1.014)
  starting transfers between devices: 11 us -> 13.4 us
  waiting for transfers between devices: 31.8 us -> 30.6 us
  Pallas kernels: 6.44 us -> 5.92 us
    ppermute x5 -> x9, waiting for transfers between devices: 21.4 us -> 8.28 us  [the longest x4 3.49 us: give_back(): lax.ppermute(cut, ('parts', 'sub'), shifted((parts, subs), (parts - e, f)))]
    ppermute x3, waiting for transfers between devices: 10.4 us -> 22.3 us  [shards(): slots[j] = lax.ppermute(sent_slots[j - 1], 'shard', to)]
    ppermute x5 -> x9, starting transfers between devices: 6.65 us -> 8.99 us  [the longest x4 3.65 us: give_back(): lax.ppermute(cut, ('parts', 'sub'), shifted((parts, subs), (parts - e, f)))]
    pallas_call x1, Pallas kernels: 2.24 us -> 1.72 us  [make_sends(): pl.pallas_call(functools.partial(send_kernel, parts, shard_count), out_sh...]
  transfers between devices with their start and end apart: 8 -> 12, of which waited for: 6 -> 9; matrix products, arithmetic and copies ran while one was open for 0% -> 0% of each run, Pallas kernels for 6% -> 6%
where the time goes in v1:
time: 51.2 us; the launch traced here: 50.5 us
  waiting for transfers between devices  30.6 us (60%)
  starting transfers between devices  13.4 us (26%)
  Pallas kernels  5.92 us (12%)
  other arithmetic  0.6 us (1%)
    ppermute x3, waiting for transfers between devices, shards(): slots[j] = lax.ppermute(sent_slots[j - 1], 'shard', to)  22.3 us
    ppermute x3, starting transfers between devices, shards(): slots[j] = lax.ppermute(sent_slots[j - 1], 'shard', to)  4.39 us
    ppermute x4, starting transfers between devices, give_back(): lax.ppermute(cut, ('parts', 'sub'), shifted((parts, subs), (parts - e, f)))  3.65 us
    ppermute x4, waiting for transfers between devices, give_back(): lax.ppermute(cut, ('parts', 'sub'), shifted((parts, subs), (parts - e, f)))  3.49 us
    ppermute x1, starting transfers between devices, shards(): lax.ppermute(sent_rows[e - 1], 'parts', shifted((parts,), (e,)))  3.06 us
    ppermute x3, waiting for transfers between devices, shards(): lax.ppermute(blocks[e], ('layer', 'sub'), shifted((layers, subs), (e, f)))  2.41 us
    ppermute x1, waiting for transfers between devices, shards(): lax.ppermute(sent_rows[e - 1], 'parts', shifted((parts,), (e,)))  2.37 us
    pallas_call x3, Pallas kernels, project(): pl.pallas_call(functools.partial(project_kernel, len(slots), len(blocks),...  2.27 us
  transfers between devices with their start and end apart: 12, of which 9 were waited for; matrix products, arithmetic and copies ran while one was open for 0% of the time, Pallas kernels for 6%

profile of v1, /device:TPU:0, one launch (start us, length us, event | category | flops | bytes accessed | tf_op | source)
XLA Modules:
  0.0 50.5 jit_solution(3571538198163863218)
XLA Ops:
  0.0 1.7 %make_sends.1 = (bf16[32,5632]{1,0:T(8,128)(2,1)S(1)}, bf16[32,5632]{1,0:T(8,128)(2,1)S(1)}, bf16[32,5632]{1,0:T(8,128)(2,1)S(1)}, bf16[128,5632]{1,0:T(8,128)(2,1)S(1)}) custom-call(s32[12]{0:T(128)} %query_hbm.3, s32[2,4,12]{2,1,0:T(4,128)} %pairs_hbm.3, bf16[1,128,7168]{2,1,0:T(8,128)(2,1)} %act.3, bf16[1,128,4096]{2,1,0:T(8,128)(2,1)} %grad.3, ...), custom_call_target="tpu_custom_call" | custom-call | tf_op jit(solution)/shard_map/make_sends/pallas_call | solution.py:106
  1.7 3.1 %collective-permute-start.2 = (bf16[128,5632]{1,0:T(8,128)(2,1)S(1)}, bf16[128,5632]{1,0:T(8,128)(2,1)S(1)}, u32[]{:S(2)}, u32[]{:S(2)}) collective-permute-start(bf16[128,5632]{1,0:T(8,128)(2,1)S(1)} %get-tuple-element.26), channel_id=1, source_target_pairs={{0,16},{16,0},{1,17},{17,1},{2,18},{18,2},{3,19},{19,3},{4,20},{20... | collective-permute-start | bytes 4325384 | tf_op jit(solution)/shard_map/ppermute | solution.py:276
  4.8 1.6 %collective-permute-start.3 = (bf16[32,5632]{1,0:T(8,128)(2,1)S(1)}, bf16[32,5632]{1,0:T(8,128)(2,1)S(1)}, u32[]{:S(2)}, u32[]{:S(2)}) collective-permute-start(bf16[32,5632]{1,0:T(8,128)(2,1)S(1)} %get-tuple-element.28), channel_id=1, source_target_pairs={{0,4},{4,0},{8,12},{12,8},{1,5},{5,1},{9,13},{13,9},{2,6},{6,2},{1... | collective-permute-start | bytes 1081352 | tf_op jit(solution)/shard_map/ppermute | solution.py:280
  6.4 2.6 %collective-permute-start = (bf16[32,5632]{1,0:T(8,128)(2,1)S(1)}, bf16[32,5632]{1,0:T(8,128)(2,1)S(1)}, u32[]{:S(2)}, u32[]{:S(2)}) collective-permute-start(bf16[32,5632]{1,0:T(8,128)(2,1)S(1)} %get-tuple-element.23), channel_id=1, source_target_pairs={{0,8},{4,12},{8,0},{12,4},{1,9},{5,13},{9,1},{13,5},{2,10},{6,14},... | collective-permute-start | bytes 1081352 | tf_op jit(solution)/shard_map/ppermute | solution.py:280
  9.0 0.2 collective-permute-start.1
  9.2 1.9 %make_own.1 = (bf16[128,5632]{1,0:T(8,128)(2,1)S(1)}, bf16[32,5632]{1,0:T(8,128)(2,1)S(1)}, f32[2,4,6,128]{3,2,1,0:T(8,128)S(1)}) custom-call(s32[12]{0:T(128)} %query_hbm.3, s32[2,4,12]{2,1,0:T(4,128)} %pairs_hbm.3, bf16[1,128,7168]{2,1,0:T(8,128)(2,1)} %act.3, bf16[1,128,4096]{2,1,0:T(8,128)(2,1)} %grad.3, bf16[1,3,32,7168]{3,2,1,0:T(8,128)(2,1)} %factor_in.3, ...), custom_call_target="tpu_custom_call" | custom-call | tf_op jit(solution)/shard_map/make_own/pallas_call | solution.py:171
  11.1 10.4 %collective-permute-done.3.refs_1_ = bf16[32,5632]{1,0:T(8,128)(2,1)S(1)} collective-permute-done((bf16[32,5632]{1,0:T(8,128)(2,1)S(1)}, bf16[32,5632]{1,0:T(8,128)(2,1)S(1)}, u32[]{:S(2)}, u32[]{:S(2)}) %collective-permute-start.3) | collective-permute-done | bytes 360480 | tf_op jit(solution)/shard_map/ppermute | solution.py:280
  21.5 0.6 %project.3 = (f32[2,2,16,128]{3,2,1,0:T(8,128)S(1)}, f32[2,2,16,128]{3,2,1,0:T(8,128)S(1)}) custom-call(bf16[32,5632]{1,0:T(8,128)(2,1)S(1)} %get-tuple-element.27.refs_0_, bf16[32,5632]{1,0:T(8,128)(2,1)S(1)} %collective-permute-done.3.refs_1_, bf16[128,5632]{1,0:T(8,128)(2,1)S(1)} %get-tuple-element.25.refs_2_), custom_call_target="tpu_custom_call" | custom-call | flops 92274688 | bytes 2162688 | tf_op jit(solution)/shard_map/project/pallas_call | solution.py:214
  22.1 11.9 %collective-permute-done.refs_0_ = bf16[32,5632]{1,0:T(8,128)(2,1)S(1)} collective-permute-done((bf16[32,5632]{1,0:T(8,128)(2,1)S(1)}, bf16[32,5632]{1,0:T(8,128)(2,1)S(1)}, u32[]{:S(2)}, u32[]{:S(2)}) %collective-permute-start) | collective-permute-done | bytes 360480 | tf_op jit(solution)/shard_map/ppermute | solution.py:280
  34.0 0.0 collective-permute-done.1.refs_1_
  34.0 2.4 %collective-permute-done.2.refs_3_.refs_2_ = bf16[128,5632]{1,0:T(8,128)(2,1)S(1)} collective-permute-done((bf16[128,5632]{1,0:T(8,128)(2,1)S(1)}, bf16[128,5632]{1,0:T(8,128)(2,1)S(1)}, u32[]{:S(2)}, u32[]{:S(2)}) %collective-permute-start.2) | collective-permute-done | bytes 1441824 | tf_op jit(solution)/shard_map/ppermute | solution.py:276
  36.4 1.1 %project.4 = (f32[2,4,16,128]{3,2,1,0:T(8,128)S(1)}, f32[2,4,16,128]{3,2,1,0:T(8,128)S(1)}, f32[2,2,16,128]{3,2,1,0:T(8,128)S(1)}, f32[2,2,16,128]{3,2,1,0:T(8,128)S(1)}) custom-call(bf16[32,5632]{1,0:T(8,128)(2,1)S(1)} %collective-permute-done.refs_0_, bf16[32,5632]{1,0:T(8,128)(2,1)S(1)} %collective-permute-done.1.refs_1_, ...), custom_call_target="tpu_custom_call" | custom-call | flops 184549376 | bytes 3604480 | tf_op jit(solution)/shard_map/project/pallas_call | solution.py:214
  37.5 0.1 collective-permute-start.4
  37.5 0.6 %project.5 = (f32[2,2,16,128]{3,2,1,0:T(8,128)S(1)}, f32[2,2,16,128]{3,2,1,0:T(8,128)S(1)}) custom-call(bf16[32,5632]{1,0:T(8,128)(2,1)S(1)} %get-tuple-element.27.refs_0_, bf16[32,5632]{1,0:T(8,128)(2,1)S(1)} %collective-permute-done.3.refs_1_, bf16[128,5632]{1,0:T(8,128)(2,1)S(1)} %collective-permute-done.2.refs_3_.refs_2_), custom_call_target="tpu_custom_call" | custom-call | flops 92274688 | bytes 2162688 | tf_op jit(solution)/shard_map/project/pallas_call | solution.py:214
  38.1 1.8 %collective-permute-start.5 = (f32[2,2,16,128]{3,2,1,0:T(8,128)S(1)}, f32[2,2,16,128]{3,2,1,0:T(8,128)S(1)}, u32[]{:S(2)}, u32[]{:S(2)}) collective-permute-start(f32[2,2,16,128]{3,2,1,0:T(8,128)S(1)} %get-tuple-element.33), channel_id=1, source_target_pairs={{0,16},{1,17},{16,0},{17,1},{2,18},{3,19},{18,2},{19,3},{4,20},{5,... | collective-permute-start | bytes 98312 | tf_op jit(solution)/shard_map/ppermute | solution.py:287
  39.9 0.2 collective-permute-start.6
  40.1 1.7 %collective-permute-start.7 = (f32[2,2,16,128]{3,2,1,0:T(8,128)S(1)}, f32[2,2,16,128]{3,2,1,0:T(8,128)S(1)}, u32[]{:S(2)}, u32[]{:S(2)}) collective-permute-start(f32[2,2,16,128]{3,2,1,0:T(8,128)S(1)} %get-tuple-element.35), channel_id=1, source_target_pairs={{0,16},{1,17},{16,0},{17,1},{2,18},{3,19},{18,2},{19,3},{4,20},{5,... | collective-permute-start | bytes 98312 | tf_op jit(solution)/shard_map/ppermute | solution.py:287
  41.8 0.0 collective-permute-start.8
  41.8 0.3 collective-permute-done.5.refs_2_
  42.1 1.2 %collective-permute-done.6.refs_3_ = f32[2,2,16,128]{3,2,1,0:T(8,128)S(1)} collective-permute-done((f32[2,2,16,128]{3,2,1,0:T(8,128)S(1)}, f32[2,2,16,128]{3,2,1,0:T(8,128)S(1)}, u32[]{:S(2)}, u32[]{:S(2)}) %collective-permute-start.6) | collective-permute-done | bytes 32800 | tf_op jit(solution)/shard_map/ppermute | solution.py:287
  43.3 1.1 %collective-permute-done.7.refs_4_ = f32[2,2,16,128]{3,2,1,0:T(8,128)S(1)} collective-permute-done((f32[2,2,16,128]{3,2,1,0:T(8,128)S(1)}, f32[2,2,16,128]{3,2,1,0:T(8,128)S(1)}, u32[]{:S(2)}, u32[]{:S(2)}) %collective-permute-start.7) | collective-permute-done | bytes 32800 | tf_op jit(solution)/shard_map/ppermute | solution.py:287
  44.3 0.9 %collective-permute-done.8.refs_5_ = f32[2,2,16,128]{3,2,1,0:T(8,128)S(1)} collective-permute-done((f32[2,2,16,128]{3,2,1,0:T(8,128)S(1)}, f32[2,2,16,128]{3,2,1,0:T(8,128)S(1)}, u32[]{:S(2)}, u32[]{:S(2)}) %collective-permute-start.8) | collective-permute-done | bytes 32800 | tf_op jit(solution)/shard_map/ppermute | solution.py:287
  45.3 0.0 collective-permute-done.4.refs_1_
  45.3 1.6 %collective-permute-start.10 = (f32[6,128]{1,0:T(8,128)S(1)}, f32[6,128]{1,0:T(8,128)S(1)}, u32[]{:S(2)}, u32[]{:S(2)}) collective-permute-start(f32[6,128]{1,0:T(8,128)S(1)} %get-tuple-element.38), channel_id=1, source_target_pairs={{0,2},{1,3},{2,0},{3,1},{4,6},{5,7},{6,4},{7,5},{8,10},{9,11},{10,... | collective-permute-start | bytes 9224 | tf_op jit(solution)/shard_map/ppermute | solution.py:302
  46.9 0.0 collective-permute-start.11
  46.9 0.6 %collective-permute-start.9 = (f32[6,128]{1,0:T(8,128)S(1)}, f32[6,128]{1,0:T(8,128)S(1)}, u32[]{:S(2)}, u32[]{:S(2)}) collective-permute-start(f32[6,128]{1,0:T(8,128)S(1)} %get-tuple-element.37), channel_id=1, source_target_pairs={{0,1},{1,0},{2,3},{3,2},{4,5},{5,4},{6,7},{7,6},{8,9},{9,8},{10,11... | collective-permute-start | bytes 9224 | tf_op jit(solution)/shard_map/ppermute | solution.py:302
  47.5 1.5 %collective-permute-done.10 = f32[6,128]{1,0:T(8,128)S(1)} collective-permute-done((f32[6,128]{1,0:T(8,128)S(1)}, f32[6,128]{1,0:T(8,128)S(1)}, u32[]{:S(2)}, u32[]{:S(2)}) %collective-permute-start.10) | collective-permute-done | bytes 3104 | tf_op jit(solution)/shard_map/ppermute | solution.py:302
  49.0 0.9 %collective-permute-done.11 = f32[6,128]{1,0:T(8,128)S(1)} collective-permute-done((f32[6,128]{1,0:T(8,128)S(1)}, f32[6,128]{1,0:T(8,128)S(1)}, u32[]{:S(2)}, u32[]{:S(2)}) %collective-permute-start.11) | collective-permute-done | bytes 3104 | tf_op jit(solution)/shard_map/ppermute | solution.py:302
  49.9 0.0 collective-permute-done.9
  49.9 0.6 %add_bitcast_fusion = f32[128,6]{0,1:T(8,128)} fusion(f32[6,128]{1,0:T(8,128)S(1)} %collective-permute-done.10, f32[6,128]{1,0:T(8,128)S(1)} %collective-permute-done.11, f32[6,128]{1,0:T(8,128)S(1)} %get-tuple-element.37, f32[6,128]{1,0:T(8,128)S(1)} %collective-permute-done.9), kind=kLoop, calls=%fused_computation | loop fusion | flops 2304 | bytes 15360 | tf_op jit(solution)/shard_map/transpose | solution.py:305
  (1 shorter events, 0.0 us)
Async XLA Ops:
  1.7 34.6 %collective-permute-start.2 = (bf16[128,5632]{1,0:T(8,128)(2,1)S(1)}, bf16[128,5632]{1,0:T(8,128)(2,1)S(1)}, u32[]{:S(2)}, u32[]{:S(2)}) collective-permute-start(bf16[128,5632]{1,0:T(8,128)(2,1)S(1)} %get-tuple-element.26), channel_id=1, source_target_pairs={{0,16},{16,0},{1,17},{17,1},{2,18},{18,2},{3,19},{19,3},{4,20},{20... | collective-permute-start | bytes 4325384 | tf_op jit(solution)/shard_map/ppermute | solution.py:276
  4.8 16.7 %collective-permute-start.3 = (bf16[32,5632]{1,0:T(8,128)(2,1)S(1)}, bf16[32,5632]{1,0:T(8,128)(2,1)S(1)}, u32[]{:S(2)}, u32[]{:S(2)}) collective-permute-start(bf16[32,5632]{1,0:T(8,128)(2,1)S(1)} %get-tuple-element.28), channel_id=1, source_target_pairs={{0,4},{4,0},{8,12},{12,8},{1,5},{5,1},{9,13},{13,9},{2,6},{6,2},{1... | collective-permute-start | bytes 1081352 | tf_op jit(solution)/shard_map/ppermute | solution.py:280
  6.4 27.6 %collective-permute-start = (bf16[32,5632]{1,0:T(8,128)(2,1)S(1)}, bf16[32,5632]{1,0:T(8,128)(2,1)S(1)}, u32[]{:S(2)}, u32[]{:S(2)}) collective-permute-start(bf16[32,5632]{1,0:T(8,128)(2,1)S(1)} %get-tuple-element.23), channel_id=1, source_target_pairs={{0,8},{4,12},{8,0},{12,4},{1,9},{5,13},{9,1},{13,5},{2,10},{6,14},... | collective-permute-start | bytes 1081352 | tf_op jit(solution)/shard_map/ppermute | solution.py:280
  9.0 25.0 %collective-permute-start.1 = (bf16[32,5632]{1,0:T(8,128)(2,1)S(1)}, bf16[32,5632]{1,0:T(8,128)(2,1)S(1)}, u32[]{:S(2)}, u32[]{:S(2)}) collective-permute-start(bf16[32,5632]{1,0:T(8,128)(2,1)S(1)} %get-tuple-element.24), channel_id=1, source_target_pairs={{0,12},{4,8},{8,4},{12,0},{1,13},{5,9},{9,5},{13,1},{2,14},{6,10},... | collective-permute-start | bytes 1081352 | tf_op jit(solution)/shard_map/ppermute | solution.py:280
  37.5 7.8 %collective-permute-start.4 = (f32[2,4,16,128]{3,2,1,0:T(8,128)S(1)}, f32[2,4,16,128]{3,2,1,0:T(8,128)S(1)}, u32[]{:S(2)}, u32[]{:S(2)}) collective-permute-start(f32[2,4,16,128]{3,2,1,0:T(8,128)S(1)} %get-tuple-element.32), channel_id=1, source_target_pairs={{0,1},{1,0},{2,3},{3,2},{4,5},{5,4},{6,7},{7,6},{8,9},{9,8},{10,11... | collective-permute-start | bytes 196616 | tf_op jit(solution)/shard_map/ppermute | solution.py:297
  38.1 4.0 %collective-permute-start.5 = (f32[2,2,16,128]{3,2,1,0:T(8,128)S(1)}, f32[2,2,16,128]{3,2,1,0:T(8,128)S(1)}, u32[]{:S(2)}, u32[]{:S(2)}) collective-permute-start(f32[2,2,16,128]{3,2,1,0:T(8,128)S(1)} %get-tuple-element.33), channel_id=1, source_target_pairs={{0,16},{1,17},{16,0},{17,1},{2,18},{3,19},{18,2},{19,3},{4,20},{5,... | collective-permute-start | bytes 98312 | tf_op jit(solution)/shard_map/ppermute | solution.py:287
  39.9 3.3 %collective-permute-start.6 = (f32[2,2,16,128]{3,2,1,0:T(8,128)S(1)}, f32[2,2,16,128]{3,2,1,0:T(8,128)S(1)}, u32[]{:S(2)}, u32[]{:S(2)}) collective-permute-start(f32[2,2,16,128]{3,2,1,0:T(8,128)S(1)} %get-tuple-element.34), channel_id=1, source_target_pairs={{0,17},{1,16},{16,1},{17,0},{2,19},{3,18},{18,3},{19,2},{4,21},{5,... | collective-permute-start | bytes 98312 | tf_op jit(solution)/shard_map/ppermute | solution.py:287
  40.1 4.2 %collective-permute-start.7 = (f32[2,2,16,128]{3,2,1,0:T(8,128)S(1)}, f32[2,2,16,128]{3,2,1,0:T(8,128)S(1)}, u32[]{:S(2)}, u32[]{:S(2)}) collective-permute-start(f32[2,2,16,128]{3,2,1,0:T(8,128)S(1)} %get-tuple-element.35), channel_id=1, source_target_pairs={{0,16},{1,17},{16,0},{17,1},{2,18},{3,19},{18,2},{19,3},{4,20},{5,... | collective-permute-start | bytes 98312 | tf_op jit(solution)/shard_map/ppermute | solution.py:287
  41.8 3.5 %collective-permute-start.8 = (f32[2,2,16,128]{3,2,1,0:T(8,128)S(1)}, f32[2,2,16,128]{3,2,1,0:T(8,128)S(1)}, u32[]{:S(2)}, u32[]{:S(2)}) collective-permute-start(f32[2,2,16,128]{3,2,1,0:T(8,128)S(1)} %get-tuple-element.36), channel_id=1, source_target_pairs={{0,17},{1,16},{16,1},{17,0},{2,19},{3,18},{18,3},{19,2},{4,21},{5,... | collective-permute-start | bytes 98312 | tf_op jit(solution)/shard_map/ppermute | solution.py:287
  45.3 3.7 %collective-permute-start.10 = (f32[6,128]{1,0:T(8,128)S(1)}, f32[6,128]{1,0:T(8,128)S(1)}, u32[]{:S(2)}, u32[]{:S(2)}) collective-permute-start(f32[6,128]{1,0:T(8,128)S(1)} %get-tuple-element.38), channel_id=1, source_target_pairs={{0,2},{1,3},{2,0},{3,1},{4,6},{5,7},{6,4},{7,5},{8,10},{9,11},{10,... | collective-permute-start | bytes 9224 | tf_op jit(solution)/shard_map/ppermute | solution.py:302
  46.9 3.1 %collective-permute-start.11 = (f32[6,128]{1,0:T(8,128)S(1)}, f32[6,128]{1,0:T(8,128)S(1)}, u32[]{:S(2)}, u32[]{:S(2)}) collective-permute-start(f32[6,128]{1,0:T(8,128)S(1)} %get-tuple-element.38), channel_id=1, source_target_pairs={{0,3},{1,2},{2,1},{3,0},{4,7},{5,6},{6,5},{7,4},{8,11},{9,10},{10,... | collective-permute-start | bytes 9224 | tf_op jit(solution)/shard_map/ppermute | solution.py:302
  46.9 3.1 %collective-permute-start.9 = (f32[6,128]{1,0:T(8,128)S(1)}, f32[6,128]{1,0:T(8,128)S(1)}, u32[]{:S(2)}, u32[]{:S(2)}) collective-permute-start(f32[6,128]{1,0:T(8,128)S(1)} %get-tuple-element.37), channel_id=1, source_target_pairs={{0,1},{1,0},{2,3},{3,2},{4,5},{5,4},{6,7},{7,6},{8,9},{9,8},{10,11... | collective-permute-start | bytes 9224 | tf_op jit(solution)/shard_map/ppermute | solution.py:302

commit v2 on v1

--- a/solution.py
+++ b/solution.py
@@ -179,62 +179,88 @@
     )(query_row, pairs, act, grad, factor_in, factor_out)
 
 
+def cut_ranks(whole, subs):
+    my_sub = lax.axis_index("sub")
+    half = whole.shape[-2] // subs
+    cuts = [whole[..., c * half : (c + 1) * half, :] for c in range(subs)]
+    picked = []
+    for f in range(subs):
+        sub = wrap(my_sub + f, subs)
+        cut = cuts[0]
+        for c in range(1, subs):
+            cut = jnp.where(sub == c, cuts[c], cut)
+        picked.append(cut)
+    return picked
+
+
 def project_kernel(slot_count, block_count, subs, wide_out, *refs):
-    slots, blocks, rest = refs[:slot_count], refs[slot_count : slot_count + block_count], refs[slot_count + block_count :]
-    carried, outs = rest[: -block_count * subs], rest[-block_count * subs :]
-    my_sub = lax.axis_index("sub")
+    slots, blocks, outs = refs[:slot_count], refs[slot_count : slot_count + block_count], refs[slot_count + block_count :]
     dims = (((1,), (1,)), ((), ()))
     rank, wide = slots[0].shape
-    half = rank // subs
-    for out, old in zip(outs, carried):
-        out[:, : old.shape[1]] = old[...]
     for which, (low, high) in enumerate(((0, wide_out), (wide_out, wide))):
         left = jnp.concatenate([slot[:, low:high] for slot in slots], axis=0)
         for e, block in enumerate(blocks):
             proj = lax.dot_general(left, block[:, low:high], dims, preferred_element_type=jnp.float32)
             for j in range(slot_count):
-                cuts = [proj[j * rank + c * half : j * rank + (c + 1) * half] for c in range(subs)]
-                for f in range(subs):
-                    sub = wrap(my_sub + f, subs)
-                    cut = cuts[0]
-                    for c in range(1, subs):
-                        cut = jnp.where(sub == c, cuts[c], cut)
-                    out = outs[e * subs + f]
-                    out[which, out.shape[1] - slot_count + j] = cut
-
-
-def project(slots, blocks, wide_out, carried=()):
-    subs = lax.axis_size("sub")
+                cuts = cut_ranks(proj[j * rank : (j + 1) * rank], subs)
+                for f, cut in enumerate(cuts):
+                    outs[e * subs + f][which, j] = cut
+
+
+def project(slots, blocks, wide_out, subs):
     vmem = pl.BlockSpec(memory_space=pltpu.VMEM)
     (rank, wide), tokens = slots[0].shape, blocks[0].shape[0]
-    counts = [len(slots) + (carried[k].shape[1] if k < len(carried) else 0) for k in range(len(blocks) * subs)]
-    inputs = [pltpu.with_memory_space_constraint(x, pltpu.VMEM) for x in (*slots, *blocks, *carried)]
+    inputs = [pltpu.with_memory_space_constraint(x, pltpu.VMEM) for x in (*slots, *blocks)]
     flops = 2 * len(slots) * rank * len(blocks) * tokens * wide
     read = 2 * wide * (len(slots) * rank + len(blocks) * tokens)
+    count = len(blocks) * subs
     return pl.pallas_call(
         functools.partial(project_kernel, len(slots), len(blocks), subs, wide_out),
-        out_shape=[pltpu.VMEM((2, count, rank // subs, tokens), jnp.float32) for count in counts],
+        out_shape=[pltpu.VMEM((2, len(slots), rank // subs, tokens), jnp.float32)] * count,
         in_specs=[vmem] * len(inputs),
-        out_specs=[vmem] * len(counts),
+        out_specs=[vmem] * count,
         compiler_params=pltpu.CompilerParams(vmem_limit_bytes=2**23),
         cost_estimate=pl.CostEstimate(flops=flops, bytes_accessed=read, transcendentals=0),
         name="project",
     )(*inputs)
 
 
-def score_kernel(counts, weights, *refs):
-    pieces, outs = list(refs[: sum(counts)]), refs[sum(counts) :]
-    whole = [pieces.pop(0) for _ in range(counts[0])]
-    scores = []
-    for count in counts[1:]:
-        parted = [pieces.pop(0) for _ in range(count)]
-        width = parted[0].shape[1]
-        total = whole[0][:, len(scores) : len(scores) + width]
-        for piece in whole[1:]:
-            total = total + piece[:, len(scores) : len(scores) + width]
-        for piece in parted:
-            total = total + piece[...]
-        scores += [jnp.sum(total[0, k] * total[1, k], axis=0, keepdims=True) for k in range(width)]
+def join_kernel(count, *refs):
+    early, late, outs = refs[:count], refs[count : count + len(refs[count:]) // 2], refs[count + len(refs[count:]) // 2 :]
+    total = early[0][...]
+    for piece in early[1:]:
+        total = total + piece[...]
+    split = total.shape[1]
+    for out, cut, rest in zip(outs, cut_ranks(total, len(outs)), late):
+        out[:, :split] = cut
+        out[:, split:] = rest[...]
+
+
+def join(early, late):
+    vmem = pl.BlockSpec(memory_space=pltpu.VMEM)
+    inputs = [pltpu.with_memory_space_constraint(x, pltpu.VMEM) for x in (*early, *late)]
+    _, count, half, tokens = late[0].shape
+    return pl.pallas_call(
+        functools.partial(join_kernel, len(early)),
+        out_shape=[pltpu.VMEM((2, early[0].shape[1] + count, half, tokens), jnp.float32)] * len(late),
+        in_specs=[vmem] * len(inputs),
+        out_specs=[vmem] * len(late),
+        compiler_params=pltpu.CompilerParams(vmem_limit_bytes=2**23),
+        name="join",
+    )(*inputs)
+
+
+def score_kernel(done, whole_count, weights, *refs):
+    layers = weights.shape[0]
+    pieces, outs = refs[:-layers], refs[-layers:]
+    whole, parted = pieces[:whole_count], pieces[whole_count:]
+    total = whole[0][...]
+    for piece in whole[1:]:
+        total = total + piece[...]
+    first, last = total[:, :done], total[:, done:]
+    for piece in parted:
+        last = last + piece[...]
+    scores = [jnp.sum(t[0, k] * t[1, k], axis=0, keepdims=True) for t in (first, last) for k in range(t.shape[1])]
     for e, out in enumerate(outs):
         block = weights[e, 0] * scores[0]
         for k in range(1, len(scores)):
@@ -243,13 +269,12 @@
 
 
 def make_scores(weights, whole, parted):
-    layers, _, wide, tokens = weights.shape
+    layers, count, wide, tokens = weights.shape
     vmem = pl.BlockSpec(memory_space=pltpu.VMEM)
-    pieces = [weights, *whole] + [piece for group in parted for piece in group]
-    inputs = [pltpu.with_memory_space_constraint(x, pltpu.VMEM) for x in pieces]
-    counts = (len(whole), *[len(group) for group in parted])
+    inputs = [pltpu.with_memory_space_constraint(x, pltpu.VMEM) for x in (weights, *whole, *parted)]
+    done = count - (parted[0].shape[1] if parted else 0)
     return pl.pallas_call(
-        functools.partial(score_kernel, counts),
+        functools.partial(score_kernel, done, len(whole)),
         out_shape=[pltpu.VMEM((wide, tokens), jnp.float32)] * layers,
         in_specs=[vmem] * len(inputs),
         out_specs=[vmem] * layers,
@@ -280,22 +305,20 @@
         slots[j] = lax.ppermute(sent_slots[j - 1], "shard", to)
     own_rows, slots[0], weights = make_own(early + late, *args)
 
-    def give_back(cuts):
-        got = []
-        for k, cut in enumerate(cuts):
-            e, f = 1 + k // subs, k % subs
-            got.append(lax.ppermute(cut, ("parts", "sub"), shifted((parts, subs), (parts - e, f))))
-        return got
-
-    early_own = project([slots[j] for j in early], [own_rows], wide_out)
-    early_rest = project([slots[j] for j in early], rows, wide_out)
-    early_got = give_back(early_rest)
-    cuts = project([slots[j] for j in late], [own_rows] + rows, wide_out, early_own)
-    late_got = give_back(cuts[subs:])
-    whole = [cuts[0]]
+    early_own = project([slots[j] for j in early], [own_rows], wide_out, 1)
+    early_rest = project([slots[j] for j in early], rows, wide_out, 1)
+    early_got = []
+    for e, block in enumerate(early_rest, 1):
+        early_got.append(lax.ppermute(block, "parts", shifted((parts,), (parts - e,))))
+    cuts = project([slots[j] for j in late], [own_rows] + rows, wide_out, subs)
+    late_got = []
+    for k, cut in enumerate(cuts[subs:]):
+        e, f = 1 + k // subs, k % subs
+        late_got.append(lax.ppermute(cut, ("parts", "sub"), shifted((parts, subs), (parts - e, f))))
+    whole = list(join(list(early_own) + early_got, cuts[:subs]))
     for f in range(1, subs):
-        whole.append(lax.ppermute(cuts[f], "sub", shifted((subs,), (f,))))
-    blocks = make_scores(weights, whole, [early_got, late_got])
+        whole[f] = lax.ppermute(whole[f], "sub", shifted((subs,), (f,)))
+    blocks = make_scores(weights, whole, late_got)
 
     out = None
     for e in range(layers):

time: 51.2 us -> 52.7 us (1.029)
  waiting for transfers between devices: 30.6 us -> 32.5 us
    ppermute x1, waiting for transfers between devices: 2.37 us -> 14.9 us  [shards(): lax.ppermute(sent_rows[e - 1], 'parts', shifted((parts,), (e,)))]
    ppermute x3, waiting for transfers between devices: 22.3 us -> 10.4 us  [shards(): slots[j] = lax.ppermute(sent_slots[j - 1], 'shard', to)]
    ppermute x3, waiting for transfers between devices: 2.41 us -> 3.07 us  [shards(): lax.ppermute(blocks[e], ('layer', 'sub'), shifted((layers, subs), (e, f)))]
    ppermute x5 -> x4, waiting for transfers between devices: 3.49 us -> 4.13 us  [the longest x2 3.31 us: shards(): lax.ppermute(cut, ('parts', 'sub'), shifted((parts, subs), (parts - e, f)))]
    ppermute x5 -> x4, starting transfers between devices: 3.72 us -> 3.72 us  [the longest x2 1.85 us: shards(): lax.ppermute(cut, ('parts', 'sub'), shifted((parts, subs), (parts - e, f)))]
  transfers between devices with their start and end apart: 12 -> 11, of which waited for: 9 -> 7; matrix products, arithmetic and copies ran while one was open for 0% -> 0% of each run, Pallas kernels for 6% -> 8%
where the time goes in v2:
time: 52.7 us; the launch traced here: 52.5 us
  waiting for transfers between devices  32.5 us (62%)
  starting transfers between devices  13.4 us (25%)
  Pallas kernels  5.93 us (11%)
  other arithmetic  0.6 us (1%)
    ppermute x1, waiting for transfers between devices, shards(): lax.ppermute(sent_rows[e - 1], 'parts', shifted((parts,), (e,)))  14.9 us
    ppermute x3, waiting for transfers between devices, shards(): slots[j] = lax.ppermute(sent_slots[j - 1], 'shard', to)  10.4 us
    ppermute x3, starting transfers between devices, shards(): slots[j] = lax.ppermute(sent_slots[j - 1], 'shard', to)  4.39 us
    ppermute x2, waiting for transfers between devices, shards(): lax.ppermute(cut, ('parts', 'sub'), shifted((parts, subs), (parts - e, f)))  3.31 us
    ppermute x3, waiting for transfers between devices, shards(): lax.ppermute(blocks[e], ('layer', 'sub'), shifted((layers, subs), (e, f)))  3.07 us
    ppermute x1, starting transfers between devices, shards(): lax.ppermute(sent_rows[e - 1], 'parts', shifted((parts,), (e,)))  3.06 us
    pallas_call x3, Pallas kernels, project(): pl.pallas_call(functools.partial(project_kernel, len(slots), len(blocks),...  2.26 us
    ppermute x3, starting transfers between devices, shards(): lax.ppermute(blocks[e], ('layer', 'sub'), shifted((layers, subs), (e, f)))  2.21 us
  transfers between devices with their start and end apart: 11, of which 7 were waited for; matrix products, arithmetic and copies ran while one was open for 0% of the time, Pallas kernels for 8%

profile of v2, /device:TPU:0, one launch (start us, length us, event | category | flops | bytes accessed | tf_op | source)
XLA Modules:
  0.0 52.5 jit_solution(9789293785912831872)
XLA Ops:
  0.0 1.7 %make_sends.1 = (bf16[32,5632]{1,0:T(8,128)(2,1)S(1)}, bf16[32,5632]{1,0:T(8,128)(2,1)S(1)}, bf16[32,5632]{1,0:T(8,128)(2,1)S(1)}, bf16[128,5632]{1,0:T(8,128)(2,1)S(1)}) custom-call(s32[12]{0:T(128)} %query_hbm.3, s32[2,4,12]{2,1,0:T(4,128)} %pairs_hbm.3, bf16[1,128,7168]{2,1,0:T(8,128)(2,1)} %act.3, bf16[1,128,4096]{2,1,0:T(8,128)(2,1)} %grad.3, ...), custom_call_target="tpu_custom_call" | custom-call | tf_op jit(solution)/shard_map/make_sends/pallas_call | solution.py:106
  1.7 3.1 %collective-permute-start.1 = (bf16[128,5632]{1,0:T(8,128)(2,1)S(1)}, bf16[128,5632]{1,0:T(8,128)(2,1)S(1)}, u32[]{:S(2)}, u32[]{:S(2)}) collective-permute-start(bf16[128,5632]{1,0:T(8,128)(2,1)S(1)} %get-tuple-element.24), channel_id=1, source_target_pairs={{0,16},{16,0},{1,17},{17,1},{2,18},{18,2},{3,19},{19,3},{4,20},{20... | collective-permute-start | bytes 4325384 | tf_op jit(solution)/shard_map/ppermute | solution.py:301
  4.8 1.6 %collective-permute-start = (bf16[32,5632]{1,0:T(8,128)(2,1)S(1)}, bf16[32,5632]{1,0:T(8,128)(2,1)S(1)}, u32[]{:S(2)}, u32[]{:S(2)}) collective-permute-start(bf16[32,5632]{1,0:T(8,128)(2,1)S(1)} %get-tuple-element.22), channel_id=1, source_target_pairs={{0,4},{4,0},{8,12},{12,8},{1,5},{5,1},{9,13},{13,9},{2,6},{6,2},{1... | collective-permute-start | bytes 1081352 | tf_op jit(solution)/shard_map/ppermute | solution.py:305
  6.4 2.6 %collective-permute-start.3 = (bf16[32,5632]{1,0:T(8,128)(2,1)S(1)}, bf16[32,5632]{1,0:T(8,128)(2,1)S(1)}, u32[]{:S(2)}, u32[]{:S(2)}) collective-permute-start(bf16[32,5632]{1,0:T(8,128)(2,1)S(1)} %get-tuple-element.25), channel_id=1, source_target_pairs={{0,8},{4,12},{8,0},{12,4},{1,9},{5,13},{9,1},{13,5},{2,10},{6,14},... | collective-permute-start | bytes 1081352 | tf_op jit(solution)/shard_map/ppermute | solution.py:305
  9.0 0.2 collective-permute-start.4
  9.2 1.9 %make_own.1 = (bf16[128,5632]{1,0:T(8,128)(2,1)S(1)}, bf16[32,5632]{1,0:T(8,128)(2,1)S(1)}, f32[2,4,6,128]{3,2,1,0:T(8,128)S(1)}) custom-call(s32[12]{0:T(128)} %query_hbm.3, s32[2,4,12]{2,1,0:T(4,128)} %pairs_hbm.3, bf16[1,128,7168]{2,1,0:T(8,128)(2,1)} %act.3, bf16[1,128,4096]{2,1,0:T(8,128)(2,1)} %grad.3, bf16[1,3,32,7168]{3,2,1,0:T(8,128)(2,1)} %factor_in.3, ...), custom_call_target="tpu_custom_call" | custom-call | tf_op jit(solution)/shard_map/make_own/pallas_call | solution.py:171
  11.1 10.4 %collective-permute-done.refs_1_ = bf16[32,5632]{1,0:T(8,128)(2,1)S(1)} collective-permute-done((bf16[32,5632]{1,0:T(8,128)(2,1)S(1)}, bf16[32,5632]{1,0:T(8,128)(2,1)S(1)}, u32[]{:S(2)}, u32[]{:S(2)}) %collective-permute-start) | collective-permute-done | bytes 360480 | tf_op jit(solution)/shard_map/ppermute | solution.py:305
  21.5 14.9 %collective-permute-done.1.refs_2_.refs_3_ = bf16[128,5632]{1,0:T(8,128)(2,1)S(1)} collective-permute-done((bf16[128,5632]{1,0:T(8,128)(2,1)S(1)}, bf16[128,5632]{1,0:T(8,128)(2,1)S(1)}, u32[]{:S(2)}, u32[]{:S(2)}) %collective-permute-start.1) | collective-permute-done | bytes 1441824 | tf_op jit(solution)/shard_map/ppermute | solution.py:301
  36.4 0.6 %project.4 = f32[2,2,32,128]{3,2,1,0:T(8,128)S(1)} custom-call(bf16[32,5632]{1,0:T(8,128)(2,1)S(1)} %get-tuple-element.21.refs_0_, bf16[32,5632]{1,0:T(8,128)(2,1)S(1)} %collective-permute-done.refs_1_, bf16[128,5632]{1,0:T(8,128)(2,1)S(1)} %collective-permute-done.1.refs_2_.refs_3_), custom_call_target="tpu_custom_call" | custom-call | flops 92274688 | bytes 2162688 | tf_op jit(solution)/shard_map/project/pallas_call | solution.py:217
  37.0 1.8 %collective-permute-start.2 = (f32[2,2,32,128]{3,2,1,0:T(8,128)S(1)}, f32[2,2,32,128]{3,2,1,0:T(8,128)S(1)}, u32[]{:S(2)}, u32[]{:S(2)}) collective-permute-start(f32[2,2,32,128]{3,2,1,0:T(8,128)S(1)} %project.4), channel_id=1, source_target_pairs={{0,16},{16,0},{1,17},{17,1},{2,18},{18,2},{3,19},{19,3},{4,20},{20... | collective-permute-start | bytes 196616 | tf_op jit(solution)/shard_map/ppermute | solution.py:312
  38.8 0.6 %project.3.refs_0_ = f32[2,2,32,128]{3,2,1,0:T(8,128)S(1)} custom-call(bf16[32,5632]{1,0:T(8,128)(2,1)S(1)} %get-tuple-element.21.refs_0_, bf16[32,5632]{1,0:T(8,128)(2,1)S(1)} %collective-permute-done.refs_1_, bf16[128,5632]{1,0:T(8,128)(2,1)S(1)} %get-tuple-element.23.refs_2_), custom_call_target="tpu_custom_call" | custom-call | flops 92274688 | bytes 2162688 | tf_op jit(solution)/shard_map/project/pallas_call | solution.py:217
  39.4 0.0 collective-permute-done.3.refs_0_
  39.4 0.0 collective-permute-done.4.refs_1_
  39.4 1.1 %project.5 = (f32[2,2,16,128]{3,2,1,0:T(8,128)S(1)}, f32[2,2,16,128]{3,2,1,0:T(8,128)S(1)}, f32[2,2,16,128]{3,2,1,0:T(8,128)S(1)}, f32[2,2,16,128]{3,2,1,0:T(8,128)S(1)}) custom-call(bf16[32,5632]{1,0:T(8,128)(2,1)S(1)} %collective-permute-done.3.refs_0_, bf16[32,5632]{1,0:T(8,128)(2,1)S(1)} %collective-permute-done.4.refs_1_, ...), custom_call_target="tpu_custom_call" | custom-call | flops 184549376 | bytes 3604480 | tf_op jit(solution)/shard_map/project/pallas_call | solution.py:217
  40.5 0.8 %collective-permute-done.2.refs_1_ = f32[2,2,32,128]{3,2,1,0:T(8,128)S(1)} collective-permute-done((f32[2,2,32,128]{3,2,1,0:T(8,128)S(1)}, f32[2,2,32,128]{3,2,1,0:T(8,128)S(1)}, u32[]{:S(2)}, u32[]{:S(2)}) %collective-permute-start.2) | collective-permute-done | bytes 65568 | tf_op jit(solution)/shard_map/ppermute | solution.py:312
  41.3 0.1 collective-permute-start.5
  41.4 1.8 %collective-permute-start.6 = (f32[2,2,16,128]{3,2,1,0:T(8,128)S(1)}, f32[2,2,16,128]{3,2,1,0:T(8,128)S(1)}, u32[]{:S(2)}, u32[]{:S(2)}) collective-permute-start(f32[2,2,16,128]{3,2,1,0:T(8,128)S(1)} %get-tuple-element.31), channel_id=1, source_target_pairs={{0,16},{1,17},{16,0},{17,1},{2,18},{3,19},{18,2},{19,3},{4,20},{5,... | collective-permute-start | bytes 98312 | tf_op jit(solution)/shard_map/ppermute | solution.py:317
  43.2 0.0 collective-permute-start.7
  43.3 2.1 %collective-permute-done.6.refs_2_ = f32[2,2,16,128]{3,2,1,0:T(8,128)S(1)} collective-permute-done((f32[2,2,16,128]{3,2,1,0:T(8,128)S(1)}, f32[2,2,16,128]{3,2,1,0:T(8,128)S(1)}, u32[]{:S(2)}, u32[]{:S(2)}) %collective-permute-start.6) | collective-permute-done | bytes 32800 | tf_op jit(solution)/shard_map/ppermute | solution.py:317
  45.4 1.2 %collective-permute-done.7.refs_3_ = f32[2,2,16,128]{3,2,1,0:T(8,128)S(1)} collective-permute-done((f32[2,2,16,128]{3,2,1,0:T(8,128)S(1)}, f32[2,2,16,128]{3,2,1,0:T(8,128)S(1)}, u32[]{:S(2)}, u32[]{:S(2)}) %collective-permute-start.7) | collective-permute-done | bytes 32800 | tf_op jit(solution)/shard_map/ppermute | solution.py:317
  46.6 0.0 collective-permute-done.5.refs_1_
  46.6 1.3 %collective-permute-start.10 = (f32[6,128]{1,0:T(8,128)S(1)}, f32[6,128]{1,0:T(8,128)S(1)}, u32[]{:S(2)}, u32[]{:S(2)}) collective-permute-start(f32[6,128]{1,0:T(8,128)S(1)} %get-tuple-element.34), channel_id=1, source_target_pairs={{0,3},{1,2},{2,1},{3,0},{4,7},{5,6},{6,5},{7,4},{8,11},{9,10},{10,... | collective-permute-start | bytes 9224 | tf_op jit(solution)/shard_map/ppermute | solution.py:325
  47.9 0.4 collective-permute-start.8
  48.3 0.5 %collective-permute-start.9 = (f32[6,128]{1,0:T(8,128)S(1)}, f32[6,128]{1,0:T(8,128)S(1)}, u32[]{:S(2)}, u32[]{:S(2)}) collective-permute-start(f32[6,128]{1,0:T(8,128)S(1)} %get-tuple-element.34), channel_id=1, source_target_pairs={{0,2},{1,3},{2,0},{3,1},{4,6},{5,7},{6,4},{7,5},{8,10},{9,11},{10,... | collective-permute-start | bytes 9224 | tf_op jit(solution)/shard_map/ppermute | solution.py:325
  48.8 0.9 %collective-permute-done.10 = f32[6,128]{1,0:T(8,128)S(1)} collective-permute-done((f32[6,128]{1,0:T(8,128)S(1)}, f32[6,128]{1,0:T(8,128)S(1)}, u32[]{:S(2)}, u32[]{:S(2)}) %collective-permute-start.10) | collective-permute-done | bytes 3104 | tf_op jit(solution)/shard_map/ppermute | solution.py:325
  49.7 0.0 collective-permute-done.8
  49.7 2.2 %collective-permute-done.9 = f32[6,128]{1,0:T(8,128)S(1)} collective-permute-done((f32[6,128]{1,0:T(8,128)S(1)}, f32[6,128]{1,0:T(8,128)S(1)}, u32[]{:S(2)}, u32[]{:S(2)}) %collective-permute-start.9) | collective-permute-done | bytes 3104 | tf_op jit(solution)/shard_map/ppermute | solution.py:325
  51.9 0.6 %add_bitcast_fusion = f32[128,6]{0,1:T(8,128)} fusion(f32[6,128]{1,0:T(8,128)S(1)} %collective-permute-done.9, f32[6,128]{1,0:T(8,128)S(1)} %collective-permute-done.10, f32[6,128]{1,0:T(8,128)S(1)} %get-tuple-element.33, f32[6,128]{1,0:T(8,128)S(1)} %collective-permute-done.8), kind=kLoop, calls=%fused_computation | loop fusion | flops 2304 | bytes 15360 | tf_op jit(solution)/shard_map/transpose | solution.py:328
  (2 shorter events, 0.0 us)
Async XLA Ops:
  1.7 34.6 %collective-permute-start.1 = (bf16[128,5632]{1,0:T(8,128)(2,1)S(1)}, bf16[128,5632]{1,0:T(8,128)(2,1)S(1)}, u32[]{:S(2)}, u32[]{:S(2)}) collective-permute-start(bf16[128,5632]{1,0:T(8,128)(2,1)S(1)} %get-tuple-element.24), channel_id=1, source_target_pairs={{0,16},{16,0},{1,17},{17,1},{2,18},{18,2},{3,19},{19,3},{4,20},{20... | collective-permute-start | bytes 4325384 | tf_op jit(solution)/shard_map/ppermute | solution.py:301
  4.8 16.7 %collective-permute-start = (bf16[32,5632]{1,0:T(8,128)(2,1)S(1)}, bf16[32,5632]{1,0:T(8,128)(2,1)S(1)}, u32[]{:S(2)}, u32[]{:S(2)}) collective-permute-start(bf16[32,5632]{1,0:T(8,128)(2,1)S(1)} %get-tuple-element.22), channel_id=1, source_target_pairs={{0,4},{4,0},{8,12},{12,8},{1,5},{5,1},{9,13},{13,9},{2,6},{6,2},{1... | collective-permute-start | bytes 1081352 | tf_op jit(solution)/shard_map/ppermute | solution.py:305
  6.4 33.0 %collective-permute-start.3 = (bf16[32,5632]{1,0:T(8,128)(2,1)S(1)}, bf16[32,5632]{1,0:T(8,128)(2,1)S(1)}, u32[]{:S(2)}, u32[]{:S(2)}) collective-permute-start(bf16[32,5632]{1,0:T(8,128)(2,1)S(1)} %get-tuple-element.25), channel_id=1, source_target_pairs={{0,8},{4,12},{8,0},{12,4},{1,9},{5,13},{9,1},{13,5},{2,10},{6,14},... | collective-permute-start | bytes 1081352 | tf_op jit(solution)/shard_map/ppermute | solution.py:305
  9.0 30.4 %collective-permute-start.4 = (bf16[32,5632]{1,0:T(8,128)(2,1)S(1)}, bf16[32,5632]{1,0:T(8,128)(2,1)S(1)}, u32[]{:S(2)}, u32[]{:S(2)}) collective-permute-start(bf16[32,5632]{1,0:T(8,128)(2,1)S(1)} %get-tuple-element.26), channel_id=1, source_target_pairs={{0,12},{4,8},{8,4},{12,0},{1,13},{5,9},{9,5},{13,1},{2,14},{6,10},... | collective-permute-start | bytes 1081352 | tf_op jit(solution)/shard_map/ppermute | solution.py:305
  37.0 4.3 %collective-permute-start.2 = (f32[2,2,32,128]{3,2,1,0:T(8,128)S(1)}, f32[2,2,32,128]{3,2,1,0:T(8,128)S(1)}, u32[]{:S(2)}, u32[]{:S(2)}) collective-permute-start(f32[2,2,32,128]{3,2,1,0:T(8,128)S(1)} %project.4), channel_id=1, source_target_pairs={{0,16},{16,0},{1,17},{17,1},{2,18},{18,2},{3,19},{19,3},{4,20},{20... | collective-permute-start | bytes 196616 | tf_op jit(solution)/shard_map/ppermute | solution.py:312
  41.3 5.2 %collective-permute-start.5 = (f32[2,4,16,128]{3,2,1,0:T(8,128)S(1)}, f32[2,4,16,128]{3,2,1,0:T(8,128)S(1)}, u32[]{:S(2)}, u32[]{:S(2)}) collective-permute-start(f32[2,4,16,128]{3,2,1,0:T(8,128)S(1)} %get-tuple-element.30), channel_id=1, source_target_pairs={{0,1},{1,0},{2,3},{3,2},{4,5},{5,4},{6,7},{7,6},{8,9},{9,8},{10,11... | collective-permute-start | bytes 196616 | tf_op jit(solution)/shard_map/ppermute | solution.py:320
  41.4 4.0 %collective-permute-start.6 = (f32[2,2,16,128]{3,2,1,0:T(8,128)S(1)}, f32[2,2,16,128]{3,2,1,0:T(8,128)S(1)}, u32[]{:S(2)}, u32[]{:S(2)}) collective-permute-start(f32[2,2,16,128]{3,2,1,0:T(8,128)S(1)} %get-tuple-element.31), channel_id=1, source_target_pairs={{0,16},{1,17},{16,0},{17,1},{2,18},{3,19},{18,2},{19,3},{4,20},{5,... | collective-permute-start | bytes 98312 | tf_op jit(solution)/shard_map/ppermute | solution.py:317
  43.2 3.4 %collective-permute-start.7 = (f32[2,2,16,128]{3,2,1,0:T(8,128)S(1)}, f32[2,2,16,128]{3,2,1,0:T(8,128)S(1)}, u32[]{:S(2)}, u32[]{:S(2)}) collective-permute-start(f32[2,2,16,128]{3,2,1,0:T(8,128)S(1)} %get-tuple-element.32), channel_id=1, source_target_pairs={{0,17},{1,16},{16,1},{17,0},{2,19},{3,18},{18,3},{19,2},{4,21},{5,... | collective-permute-start | bytes 98312 | tf_op jit(solution)/shard_map/ppermute | solution.py:317
  46.6 3.1 %collective-permute-start.10 = (f32[6,128]{1,0:T(8,128)S(1)}, f32[6,128]{1,0:T(8,128)S(1)}, u32[]{:S(2)}, u32[]{:S(2)}) collective-permute-start(f32[6,128]{1,0:T(8,128)S(1)} %get-tuple-element.34), channel_id=1, source_target_pairs={{0,3},{1,2},{2,1},{3,0},{4,7},{5,6},{6,5},{7,4},{8,11},{9,10},{10,... | collective-permute-start | bytes 9224 | tf_op jit(solution)/shard_map/ppermute | solution.py:325
  47.9 1.8 %collective-permute-start.8 = (f32[6,128]{1,0:T(8,128)S(1)}, f32[6,128]{1,0:T(8,128)S(1)}, u32[]{:S(2)}, u32[]{:S(2)}) collective-permute-start(f32[6,128]{1,0:T(8,128)S(1)} %get-tuple-element.33), channel_id=1, source_target_pairs={{0,1},{1,0},{2,3},{3,2},{4,5},{5,4},{6,7},{7,6},{8,9},{9,8},{10,11... | collective-permute-start | bytes 9224 | tf_op jit(solution)/shard_map/ppermute | solution.py:325
  48.3 3.6 %collective-permute-start.9 = (f32[6,128]{1,0:T(8,128)S(1)}, f32[6,128]{1,0:T(8,128)S(1)}, u32[]{:S(2)}, u32[]{:S(2)}) collective-permute-start(f32[6,128]{1,0:T(8,128)S(1)} %get-tuple-element.34), channel_id=1, source_target_pairs={{0,2},{1,3},{2,0},{3,1},{4,6},{5,7},{6,4},{7,5},{8,10},{9,11},{10,... | collective-permute-start | bytes 9224 | tf_op jit(solution)/shard_map/ppermute | solution.py:325
